TPU v7x, 128 devices: a whole 4x4x4 slice. The times are simulated.
128 devices in a mesh: freq: 2 (over core), vs: 64 (over z, y, x).
Axes of the slice: x: 4, y: 4, z: 4, core: 2. Of those that a mesh axis runs over, the one named last changes fastest.
Arguments:
- kernel: bfloat16 [4, 2, 256, 16384], P('freq', None, None, 'vs'), may hold values from -0.03125 to 0.03125
- sources: bfloat16 [4, 2, 2048, 16384], P('freq', None, 'vs'), may hold values from -6 to 6
- observed: float32 [256, 160, 2048], P('freq', None, 'vs'), may hold values from -6 to 6
- gate_start: int32 [256], P('freq'), may hold values from 0 to 80, as said below
- gate_length: int32 [256], P('freq'), may hold values from 1 to 160
Outputs:
- gradient: bfloat16 [4, 2, 2048, 16384], P('freq', None, 'vs')
- misfit: float32 [256, 160, 2048], P('freq', None, 'vs')
Inputs may be any that keep to these rules, and one draw needn't show every extreme that they name: gate_start + gate_length <= 160 for every receiver.
All inputs are finite; a program needn't handle non-finite values.
Results may differ from a plain program's by a relative error of at most 0.0057.
Values may be sent and summed in bfloat16 or wider, within the bound.
No kernel may reach another device: no remote copies, remote signals or barrier semaphores. Data moves between devices by JAX's collectives and lax.ppermute only.
A program may use at most 128 MiB of HBM per device.

v0:
```python
import jax
import jax.numpy as jnp
from jax import lax
from jax.sharding import PartitionSpec as P

NS = 16384
RW = 256


def complex_apply(kern, model):
    form = "frs,fvs->frv"
    real_part = jnp.einsum(
        form, kern[:, 0], model[:, 0], preferred_element_type=jnp.float32
    ) - jnp.einsum(form, kern[:, 1], model[:, 1], preferred_element_type=jnp.float32)
    imag_part = jnp.einsum(
        form, kern[:, 0], model[:, 1], preferred_element_type=jnp.float32
    ) + jnp.einsum(form, kern[:, 1], model[:, 0], preferred_element_type=jnp.float32)
    return jnp.stack([real_part, imag_part], 1)


def complex_adjoint(kern, spectrum):
    form = "frv,frs->fvs"
    real_part = jnp.einsum(
        form, spectrum[:, 0], kern[:, 0], preferred_element_type=jnp.float32
    ) + jnp.einsum(form, spectrum[:, 1], kern[:, 1], preferred_element_type=jnp.float32)
    imag_part = jnp.einsum(
        form, spectrum[:, 1], kern[:, 0], preferred_element_type=jnp.float32
    ) - jnp.einsum(form, spectrum[:, 0], kern[:, 1], preferred_element_type=jnp.float32)
    factor = (NS / RW) ** 0.5
    return factor * jnp.stack([real_part, imag_part], 1)


def transform_tables(count, samples):
    sample_index = jnp.arange(samples, dtype=jnp.int32)
    bin_index = samples // 4 + jnp.arange(count, dtype=jnp.int32)
    phase = sample_index[:, None] * bin_index[None, :] % samples
    theta = 2.0 * jnp.pi / samples * phase.astype(jnp.float32)
    return (jnp.cos(theta), jnp.sin(theta))


def local(kernel, sources, observed, gate_start, gate_length):
    gathered = lax.all_gather(kernel, "vs", axis=3, tiled=True)
    forward = complex_apply(gathered, sources)
    field = forward.astype(jnp.bfloat16)
    timed = lax.all_to_all(field, "freq", split_axis=2, concat_axis=0, tiled=True)
    count = timed.shape[0]
    samples = observed.shape[1]
    cosine, sine = transform_tables(count, samples)
    scale = count ** (-0.5)
    values = timed.astype(jnp.float32)
    highest = lax.Precision.HIGHEST
    signal = scale * (
        jnp.einsum("tf,frv->rtv", cosine, values[:, 0], precision=highest)
        - jnp.einsum("tf,frv->rtv", sine, values[:, 1], precision=highest)
    )
    sample_index = jnp.arange(samples, dtype=jnp.int32)
    inside = (sample_index[None, :] >= gate_start[:, None]) & (
        sample_index[None, :] < (gate_start + gate_length)[:, None]
    )
    gate_mask = inside.astype(jnp.float32)
    misfit = gate_mask[:, :, None] * (signal - observed)
    back_real = scale * jnp.einsum("tf,rtv->frv", cosine, misfit, precision=highest)
    back_imag = -scale * jnp.einsum("tf,rtv->frv", sine, misfit, precision=highest)
    back_spectrum = jnp.stack([back_real, back_imag], 1).astype(jnp.bfloat16)
    spectral = lax.all_to_all(back_spectrum, "freq", split_axis=0, concat_axis=2, tiled=True)
    gradient = complex_adjoint(gathered, spectral).astype(jnp.bfloat16)
    return (gradient, misfit)


def solution(mesh):
    return jax.shard_map(
        local,
        mesh=mesh,
        in_specs=(
            P("freq", None, None, "vs"),
            P("freq", None, "vs", None),
            P("freq", None, "vs"),
            P("freq"),
            P("freq"),
        ),
        out_specs=(P("freq", None, "vs", None), P("freq", None, "vs")),
        check_vma=False,
    )
```

profile of v0, /device:TPU:1, one launch (start us, length us, event | category | flops | bytes accessed | tf_op | source)
XLA Modules:
  0.0 335.3 jit_solution(14792505252984407137)
XLA Ops:
  7.2 0.0 all-gather.2.cloned.1.call-start
  7.2 1.9 copy.15
  9.1 0.0 all-gather.2.cloned.1.call-update
  9.1 0.7 add.36
  9.8 0.7 fusion.41
  10.5 229.3 %all-gather.2.cloned.1.call-done = bf16[2,2,256,16384]{3,2,0,1:T(8,128)(2,1)} async-done(((bf16[2,2,256,256]{3,2,0,1:T(8,128)(2,1)}), bf16[2,2,256,16384]{3,2,0,1:T(8,128)(2,1)}) %all-gather.2.cloned.1.call-update) | async-done | bytes 33554448 | tf_op jit(solution)/shard_map/all_gather | solution.py:42
  239.8 0.0 copy-start.1
  239.8 10.0 %fusion.4 = f32[2,256,32]{1,2,0:T(8,128)S(1)} fusion(bf16[2,2,256,16384]{3,2,0,1:T(8,128)(2,1)} %all-gather.2.cloned.1.call-done, bf16[2,2,32,16384]{3,2,1,0:T(8,128)(2,1)} %param.6), kind=kOutput, calls=%fused_computation.8 | convolution fusion | flops 536870912 | bytes 18939904 | tf_op jit(solution)/shard_map/frs,fvs->frv/dot_general | solution.py:15
  249.7 0.0 copy-done.1
  249.7 8.6 %fusion.5 = f32[2,256,32]{1,2,0:T(8,128)S(1)} fusion(bf16[2,2,256,16384]{3,2,0,1:T(8,128)(2,1)} %all-gather.2.cloned.1.call-done, bf16[2,2,32,16384]{3,2,1,0:T(8,128)(2,1)S(1)} %copy-done.1), kind=kOutput, calls=%fused_computation.9 | convolution fusion | flops 536870912 | bytes 18939904 | tf_op jit(solution)/shard_map/frs,fvs->frv/dot_general | solution.py:12
  258.4 8.6 %fusion.37 = bf16[2,1,256,32]{2,3,0,1:T(8,128)(2,1)S(1)} fusion(f32[2,256,32]{1,2,0:T(8,128)S(1)} %fusion.4, bf16[2,2,32,16384]{3,2,1,0:T(8,128)(2,1)S(1)} %copy-done.1, bf16[2,2,256,16384]{3,2,0,1:T(8,128)(2,1)} %all-gather.2.cloned.1.call-done), kind=kOutput, calls=%fused_computation.35 | convolution fusion | flops 536903680 | bytes 18972672 | tf_op jit(solution)/shard_map/frs,fvs->frv/dot_general | solution.py:17
  267.0 8.6 %fusion.34 = bf16[2,1,256,32]{2,3,0,1:T(8,128)(2,1)S(1)} fusion(f32[2,256,32]{1,2,0:T(8,128)S(1)} %fusion.5, bf16[2,2,32,16384]{3,2,1,0:T(8,128)(2,1)S(1)} %copy-done.1, bf16[2,2,256,16384]{3,2,0,1:T(8,128)(2,1)} %all-gather.2.cloned.1.call-done), kind=kOutput, calls=%fused_computation.34 | convolution fusion | flops 536903680 | bytes 18972672 | tf_op jit(solution)/shard_map/frs,fvs->frv/dot_general | solution.py:14
  275.7 0.0 copy-start
  275.7 0.2 copy.18
  275.9 0.3 reshape.54
  276.2 5.6 %all_to_all.36 = bf16[2,2,8192]{2,1,0:T(2,128)(2,1)S(1)} all-to-all(bf16[2,2,8192]{2,1,0:T(2,128)(2,1)S(1)} %reshape.54), channel_id=1, replica_groups=mesh['freq'=2,'vs'=64] {'freq'}, dimensions={0} | all-to-all | bytes 131072 | tf_op jit(solution)/shard_map/all_to_all | solution.py:45
  281.8 0.2 reshape.55
  282.0 0.1 copy.19
  282.1 1.3 fusion.42
  283.5 0.0 copy-done
  283.5 3.0 fusion.9
  286.5 1.4 fusion.32
  287.9 1.4 fusion.33
  289.3 3.0 copy.24
  292.4 3.8 %all_to_all.37 = bf16[4,2,128,32]{2,3,1,0:T(8,128)(2,1)S(1)} all-to-all(bf16[4,2,128,32]{2,3,1,0:T(8,128)(2,1)S(1)} %copy.21), channel_id=1, replica_groups=mesh['freq'=2,'vs'=64] {'freq'}, dimensions={0} | all-to-all | bytes 131072 | tf_op jit(solution)/shard_map/all_to_all | solution.py:65
  296.2 0.1 copy.29
  296.4 7.3 %fusion.2 = f32[2,32,16384]{2,1,0:T(8,128)S(1)} fusion(bf16[2,2,256,16384]{3,2,0,1:T(8,128)(2,1)} %all-gather.2.cloned.1.call-done, bf16[2,2,256,32]{2,3,0,1:T(8,128)(2,1)S(1)} %all_to_all.33), kind=kOutput, calls=%fused_computation.6 | convolution fusion | flops 536870912 | bytes 21004288 | tf_op jit(solution)/shard_map/frv,frs->fvs/dot_general | solution.py:26
  303.7 7.3 %fusion.3 = f32[2,32,16384]{2,1,0:T(8,128)S(1)} fusion(bf16[2,2,256,16384]{3,2,0,1:T(8,128)(2,1)} %all-gather.2.cloned.1.call-done, bf16[2,2,256,32]{2,3,0,1:T(8,128)(2,1)S(1)} %all_to_all.33), kind=kOutput, calls=%fused_computation.7 | convolution fusion | flops 536870912 | bytes 21004288 | tf_op jit(solution)/shard_map/frv,frs->fvs/dot_general | solution.py:23
  311.0 7.3 %fusion.1 = f32[2,1,32,16384]{3,2,0,1:T(8,128)S(1)} fusion(f32[2,32,16384]{2,1,0:T(8,128)S(1)} %fusion.2, bf16[2,2,256,16384]{3,2,0,1:T(8,128)(2,1)} %all-gather.2.cloned.1.call-done, bf16[2,2,256,32]{2,3,0,1:T(8,128)(2,1)S(1)} %all_to_all.33), kind=kOutput, calls=%fused_computation.3 | convolution fusion | flops 537919488 | bytes 25198592 | tf_op jit(solution)/shard_map/frv,frs->fvs/dot_general | solution.py:28
  318.3 7.3 %fusion = f32[2,1,32,16384]{3,2,0,1:T(8,128)S(1)} fusion(f32[2,32,16384]{2,1,0:T(8,128)S(1)} %fusion.3, bf16[2,2,256,16384]{3,2,0,1:T(8,128)(2,1)} %all-gather.2.cloned.1.call-done, bf16[2,2,256,32]{2,3,0,1:T(8,128)(2,1)S(1)} %all_to_all.33), kind=kOutput, calls=%fused_computation.2 | convolution fusion | flops 537919488 | bytes 25198592 | tf_op jit(solution)/shard_map/frv,frs->fvs/dot_general | solution.py:25
  325.7 0.5 fusion.8
  326.2 2.3 copy.23
  (5 shorter events, 0.1 us)
Async XLA Ops:
  7.2 232.6 %all-gather.2.cloned.1.call-start = ((), (), s32[]{:S(2)}) async-start(), calls=%async_computation.2 | async-start | bytes 34078720 | tf_op jit(solution)/shard_map/all_gather | solution.py:42
  239.8 10.0 %copy-start.1 = (bf16[2,2,32,16384]{3,2,1,0:T(8,128)(2,1)S(1)}, bf16[2,2,32,16384]{3,2,1,0:T(8,128)(2,1)}, u32[]{:S(2)}) copy-start(bf16[2,2,32,16384]{3,2,1,0:T(8,128)(2,1)} %param.6) | copy-start | bytes 12582916
  275.7 7.8 %copy-start = (f32[128,160,32]{0,2,1:T(8,128)S(1)}, f32[128,160,32]{0,2,1:T(8,128)}, u32[]{:S(2)}) copy-start(f32[128,160,32]{0,2,1:T(8,128)} %param.7) | copy-start | bytes 7864324
Sparse Core Ops, SparseCore 0:
  11.2 228.4 all-gather.1
where the time goes:
time: 336 us; the launch traced here: 335 us
  waiting for transfers between devices  229 us (68%)
  matrix products  72.3 us (22%)
  between operations  14.2 us (4%)
  blocking collectives  9.47 us (3%)
  local copies, waits for them, and re-layouts  8.13 us (2%)
    all_gather x1, waiting for transfers between devices, local(): gathered = lax.all_gather(kernel, 'vs', axis=3, tiled=True)  229 us
    dot_general x1, matrix products, complex_apply(): jnp.einsum(form, kern[:, 0], model[:, 1], preferred_element_type=jnp.floa...  9.96 us
    dot_general x1, matrix products, complex_apply(): jnp.einsum(form, kern[:, 1], model[:, 0], preferred_element_type=jnp.floa...  8.64 us
    dot_general x1, matrix products, complex_apply(): jnp.einsum(form, kern[:, 1], model[:, 1], preferred_element_type=jnp.floa...  8.64 us
    dot_general x1, matrix products, complex_apply(): jnp.einsum(form, kern[:, 0], model[:, 0], preferred_element_type=jnp.floa...  8.62 us
    unnamed x9, local copies, waits for them, and re-layouts  7.7 us
    dot_general x1, matrix products, complex_adjoint(): jnp.einsum(form, spectrum[:, 0], kern[:, 1], preferred_element_type=jnp.f...  7.33 us
    dot_general x1, matrix products, complex_adjoint(): jnp.einsum(form, spectrum[:, 1], kern[:, 1], preferred_element_type=jnp.f...  7.33 us
  transfers between devices with their start and end apart: 1, of which 1 were waited for; matrix products, arithmetic and copies ran while one was open for 0% of the time, Pallas kernels for 0%

commit v1 on v0

--- a/solution.py
+++ b/solution.py
@@ -39,7 +39,7 @@
 
 
 def local(kernel, sources, observed, gate_start, gate_length):
-    gathered = lax.all_gather(kernel, "vs", axis=3, tiled=True)
+    gathered = jnp.concatenate(lax.all_gather(kernel, "vs"), axis=3)
     forward = complex_apply(gathered, sources)
     field = forward.astype(jnp.bfloat16)
     timed = lax.all_to_all(field, "freq", split_axis=2, concat_axis=0, tiled=True)

time: 336 us -> 352 us (1.048)
  local copies, waits for them, and re-layouts: 8.13 us -> 87.4 us
  waiting for transfers between devices: 229 us -> 166 us
    all_gather x1, waiting for transfers between devices: 229 us -> 165 us  [local(): gathered = jnp.concatenate(lax.all_gather(kernel, 'vs'), axis=3)]
    reshape x0 -> x1, local copies, waits for them, and re-layouts: none -> 49.9 us  [local(): gathered = jnp.concatenate(lax.all_gather(kernel, 'vs'), axis=3)]
    all_gather x0 -> x1, local copies, waits for them, and re-layouts: none -> 31.3 us  [local(): gathered = jnp.concatenate(lax.all_gather(kernel, 'vs'), axis=3)]
    unnamed x9 -> x8, local copies, waits for them, and re-layouts: 7.7 us -> 5.83 us
where the time goes in v1:
time: 352 us; the launch traced here: 350 us
  waiting for transfers between devices  166 us (47%)
  local copies, waits for them, and re-layouts  87.4 us (25%)
  matrix products  72.3 us (21%)
  between operations  14.2 us (4%)
  blocking collectives  8.28 us (2%)
    all_gather x1, waiting for transfers between devices, local(): gathered = jnp.concatenate(lax.all_gather(kernel, 'vs'), axis=3)  165 us
    reshape x1, local copies, waits for them, and re-layouts, local(): gathered = jnp.concatenate(lax.all_gather(kernel, 'vs'), axis=3)  49.9 us
    all_gather x1, local copies, waits for them, and re-layouts, local(): gathered = jnp.concatenate(lax.all_gather(kernel, 'vs'), axis=3)  31.3 us
    dot_general x1, matrix products, complex_apply(): jnp.einsum(form, kern[:, 0], model[:, 1], preferred_element_type=jnp.floa...  9.96 us
    dot_general x1, matrix products, complex_apply(): jnp.einsum(form, kern[:, 1], model[:, 1], preferred_element_type=jnp.floa...  8.64 us
    dot_general x1, matrix products, complex_apply(): jnp.einsum(form, kern[:, 1], model[:, 0], preferred_element_type=jnp.floa...  8.64 us
    dot_general x1, matrix products, complex_apply(): jnp.einsum(form, kern[:, 0], model[:, 0], preferred_element_type=jnp.floa...  8.62 us
    dot_general x1, matrix products, complex_adjoint(): jnp.einsum(form, spectrum[:, 0], kern[:, 1], preferred_element_type=jnp.f...  7.33 us
  transfers between devices with their start and end apart: 1, of which 1 were waited for; matrix products, arithmetic and copies ran while one was open for 0% of the time, Pallas kernels for 0%

profile of v1, /device:TPU:1, one launch (start us, length us, event | category | flops | bytes accessed | tf_op | source)
XLA Modules:
  0.0 350.0 jit_solution(8827043360132575053)
XLA Ops:
  7.2 0.0 all-gather.3.cloned.1.call-start
  7.2 0.7 all-gather.3.cloned.1.call-update
  7.9 0.7 add.36
  8.6 0.7 fusion.41
  9.3 165.2 %all-gather.3.cloned.1.call-done = bf16[128,2,256,256]{3,2,1,0:T(8,128)(2,1)} async-done(((bf16[2,2,256,256]{3,2,1,0:T(8,128)(2,1)}), bf16[128,2,256,256]{3,2,1,0:T(8,128)(2,1)}) %all-gather.3.cloned.1.call-update) | async-done | bytes 33554448 | tf_op jit(solution)/shard_map/all_gather | solution.py:42
  174.5 31.3 %copy.30 = bf16[64,2,2,256,256]{4,0,3,1,2:T(8,128)(2,1)} copy(bf16[64,2,2,256,256]{4,3,2,1,0:T(8,128)(2,1)} %bitcast.113) | data formatting | bytes 67108864 | tf_op jit(solution)/shard_map/all_gather | solution.py:42
  205.8 49.9 %reshape.59 = bf16[2,2,256,16384]{3,2,0,1:T(8,128)(2,1)} reshape(bf16[2,2,256,64,256]{4,3,2,0,1:T(8,128)(2,1)} %bitcast.112) | data formatting | bytes 67108864 | tf_op jit(solution)/shard_map/reshape | solution.py:42
  255.7 0.0 copy-start.1
  255.7 10.0 %fusion.4 = f32[2,256,32]{1,2,0:T(8,128)S(1)} fusion(bf16[2,2,256,16384]{3,2,0,1:T(8,128)(2,1)} %reshape.59, bf16[2,2,32,16384]{3,2,1,0:T(8,128)(2,1)} %param.6), kind=kOutput, calls=%fused_computation.9 | convolution fusion | flops 536870912 | bytes 18939904 | tf_op jit(solution)/shard_map/frs,fvs->frv/dot_general | solution.py:15
  265.6 0.0 copy-done.1
  265.6 8.6 %fusion.5 = f32[2,256,32]{1,2,0:T(8,128)S(1)} fusion(bf16[2,2,256,16384]{3,2,0,1:T(8,128)(2,1)} %reshape.59, bf16[2,2,32,16384]{3,2,1,0:T(8,128)(2,1)S(1)} %copy-done.1), kind=kOutput, calls=%fused_computation.10 | convolution fusion | flops 536870912 | bytes 18939904 | tf_op jit(solution)/shard_map/frs,fvs->frv/dot_general | solution.py:12
  274.3 8.6 %fusion.37 = bf16[2,1,256,32]{2,3,0,1:T(8,128)(2,1)S(1)} fusion(f32[2,256,32]{1,2,0:T(8,128)S(1)} %fusion.4, bf16[2,2,32,16384]{3,2,1,0:T(8,128)(2,1)S(1)} %copy-done.1, bf16[2,2,256,16384]{3,2,0,1:T(8,128)(2,1)} %reshape.59), kind=kOutput, calls=%fused_computation.36 | convolution fusion | flops 536903680 | bytes 18972672 | tf_op jit(solution)/shard_map/frs,fvs->frv/dot_general | solution.py:17
  282.9 8.6 %fusion.34 = bf16[2,1,256,32]{2,3,0,1:T(8,128)(2,1)S(1)} fusion(f32[2,256,32]{1,2,0:T(8,128)S(1)} %fusion.5, bf16[2,2,32,16384]{3,2,1,0:T(8,128)(2,1)S(1)} %copy-done.1, bf16[2,2,256,16384]{3,2,0,1:T(8,128)(2,1)} %reshape.59), kind=kOutput, calls=%fused_computation.35 | convolution fusion | flops 536903680 | bytes 18972672 | tf_op jit(solution)/shard_map/frs,fvs->frv/dot_general | solution.py:14
  291.6 0.0 copy-start
  291.6 0.2 copy.18
  291.8 0.3 reshape.63
  292.1 4.4 %all_to_all.36 = bf16[2,2,8192]{2,1,0:T(2,128)(2,1)S(1)} all-to-all(bf16[2,2,8192]{2,1,0:T(2,128)(2,1)S(1)} %reshape.63), channel_id=1, replica_groups=mesh['freq'=2,'vs'=64] {'freq'}, dimensions={0} | all-to-all | bytes 131072 | tf_op jit(solution)/shard_map/all_to_all | solution.py:45
  296.5 0.2 reshape.64
  296.7 0.1 copy.19
  296.8 1.3 fusion.42
  298.2 0.0 copy-done
  298.2 3.0 fusion.9
  301.2 1.4 fusion.32
  302.6 1.4 fusion.33
  304.0 3.0 copy.24
  307.1 3.8 %all_to_all.37 = bf16[4,2,128,32]{2,3,1,0:T(8,128)(2,1)S(1)} all-to-all(bf16[4,2,128,32]{2,3,1,0:T(8,128)(2,1)S(1)} %copy.21), channel_id=1, replica_groups=mesh['freq'=2,'vs'=64] {'freq'}, dimensions={0} | all-to-all | bytes 131072 | tf_op jit(solution)/shard_map/all_to_all | solution.py:65
  310.9 0.1 copy.31
  311.1 7.3 %fusion.2 = f32[2,32,16384]{2,1,0:T(8,128)S(1)} fusion(bf16[2,2,256,16384]{3,2,0,1:T(8,128)(2,1)} %reshape.59, bf16[2,2,256,32]{2,3,0,1:T(8,128)(2,1)S(1)} %all_to_all.33), kind=kOutput, calls=%fused_computation.7 | convolution fusion | flops 536870912 | bytes 21004288 | tf_op jit(solution)/shard_map/frv,frs->fvs/dot_general | solution.py:26
  318.4 7.3 %fusion.3 = f32[2,32,16384]{2,1,0:T(8,128)S(1)} fusion(bf16[2,2,256,16384]{3,2,0,1:T(8,128)(2,1)} %reshape.59, bf16[2,2,256,32]{2,3,0,1:T(8,128)(2,1)S(1)} %all_to_all.33), kind=kOutput, calls=%fused_computation.8 | convolution fusion | flops 536870912 | bytes 21004288 | tf_op jit(solution)/shard_map/frv,frs->fvs/dot_general | solution.py:23
  325.7 7.3 %fusion.1 = f32[2,1,32,16384]{3,2,0,1:T(8,128)S(1)} fusion(f32[2,32,16384]{2,1,0:T(8,128)S(1)} %fusion.2, bf16[2,2,256,16384]{3,2,0,1:T(8,128)(2,1)} %reshape.59, bf16[2,2,256,32]{2,3,0,1:T(8,128)(2,1)S(1)} %all_to_all.33), kind=kOutput, calls=%fused_computation.4 | convolution fusion | flops 537919488 | bytes 25198592 | tf_op jit(solution)/shard_map/frv,frs->fvs/dot_general | solution.py:28
  333.0 7.3 %fusion = f32[2,1,32,16384]{3,2,0,1:T(8,128)S(1)} fusion(f32[2,32,16384]{2,1,0:T(8,128)S(1)} %fusion.3, bf16[2,2,256,16384]{3,2,0,1:T(8,128)(2,1)} %reshape.59, bf16[2,2,256,32]{2,3,0,1:T(8,128)(2,1)S(1)} %all_to_all.33), kind=kOutput, calls=%fused_computation.3 | convolution fusion | flops 537919488 | bytes 25198592 | tf_op jit(solution)/shard_map/frv,frs->fvs/dot_general | solution.py:25
  340.4 0.5 fusion.8
  340.9 2.3 copy.23
  (5 shorter events, 0.1 us)
Async XLA Ops:
  7.2 167.3 %all-gather.3.cloned.1.call-start = ((), (), s32[]{:S(2)}) async-start(), calls=%async_computation.2 | async-start | bytes 34078720 | tf_op jit(solution)/shard_map/all_gather | solution.py:42
  255.7 10.0 %copy-start.1 = (bf16[2,2,32,16384]{3,2,1,0:T(8,128)(2,1)S(1)}, bf16[2,2,32,16384]{3,2,1,0:T(8,128)(2,1)}, u32[]{:S(2)}) copy-start(bf16[2,2,32,16384]{3,2,1,0:T(8,128)(2,1)} %param.6) | copy-start | bytes 12582916
  291.6 6.6 %copy-start = (f32[128,160,32]{0,2,1:T(8,128)S(1)}, f32[128,160,32]{0,2,1:T(8,128)}, u32[]{:S(2)}) copy-start(f32[128,160,32]{0,2,1:T(8,128)} %param.7) | copy-start | bytes 7864324
Sparse Core Ops, SparseCore 0:
  10.8 163.6 all-gather.2
